TPU v7x, 32 devices: a whole 2x2x4 slice. The times are simulated.
32 devices in a mesh: ka: 16 (over z, y, core), aux: 2 (over x).
Axes of the slice: x: 2, y: 2, z: 4, core: 2. Of those that a mesh axis runs over, the one named last changes fastest.
Arguments:
- coefficients: bfloat16 [16, 4096, 128], P('ka'), may hold values from -2.09375 to 2.09375
- triple: bfloat16 [64, 2, 64, 768], P('aux'), may hold values from -0.5 to 0.5
- neighbors: int32 [64, 2], P('aux'), may hold values from 0 to 63
- w_screened: bfloat16 [16, 768, 1536], P('ka', 'aux'), as said below
- partner: int32 [2, 16], replicated, may hold values from 0 to 15, each once within a row
- q_ids: int32 [2], replicated, may hold values from 0 to 15
Outputs:
- sigma: float32 [16, 64, 128], P('ka', 'aux')
Inputs may be any that keep to these rules, and one draw needn't show every extreme that they name: Each stored w_screened is Hermitian: its real block is symmetric and its imaginary block antisymmetric.
All inputs are finite; a program needn't handle non-finite values.
Results may differ from a plain program's by a relative error of at most 0.0085.
Values may be sent and summed in bfloat16 or wider, within the bound.
A program may use at most 128 MiB of HBM per device.

v0:
```python
import math
import jax
import jax.numpy as jnp
from jax import lax
from jax.sharding import PartitionSpec as P

CELL_ATOMS = 64
ORBITALS_PER_ATOM = 64
AUX_ATOM = 12
OCCUPIED_BANDS = 16
TRANSFERS = 2
NAUX = 768


def from_root(block, axis, source):
    block = jnp.where(lax.axis_index(axis) == source, block, jnp.zeros_like(block))
    return lax.psum(block, axis)


def from_partner(value, axis, distance):
    mask = 2**distance
    pairs = [(source, source ^ mask) for source in range(lax.axis_size(axis))]
    return lax.ppermute(value, axis, pairs)


def rotated_parts(values, band_count):
    return jnp.concatenate([-values[..., band_count:], values[..., :band_count]], axis=-1)


def apply_block(weights, start, values, band_count):
    kpoints, rows, occupied, doubled = values.shape
    real_cols = lax.dynamic_slice_in_dim(weights, start, rows, 1)
    imag_cols = lax.dynamic_slice_in_dim(weights, NAUX + start, rows, 1)
    flat = values.reshape(kpoints, rows, occupied * doubled)
    turned = rotated_parts(values, band_count).reshape(kpoints, rows, occupied * doubled)
    result = jnp.einsum("ab,kbx->kax", real_cols, flat, preferred_element_type=jnp.float32)
    result = result + jnp.einsum(
        "ab,kbx->kax", imag_cols, turned, preferred_element_type=jnp.float32
    )
    return result.reshape(kpoints, weights.shape[0], occupied, doubled)


def pair_blocks(left_values, right_values):
    kpoints = left_values.shape[0]
    doubled = left_values.shape[-1]
    left_flat = left_values.reshape(kpoints, -1, doubled)
    right_flat = right_values.reshape(kpoints, -1, doubled)
    return jnp.einsum("kxm,kxn->kmn", left_flat, right_flat, preferred_element_type=jnp.float32)


def sigma_parts(blocks, band_count):
    sigma_real = blocks[:, :band_count, :band_count] + blocks[:, band_count:, band_count:]
    sigma_imag = blocks[:, :band_count, band_count:] - blocks[:, band_count:, :band_count]
    return (sigma_real, sigma_imag)


def local(coefficients, triple, neighbors, w_screened, partner, q_ids):
    kpoints, orbitals, doubled = coefficients.shape
    band_count = doubled // 2
    local_atoms = triple.shape[0]
    local_aux = local_atoms * AUX_ATOM
    half_index = lax.axis_index("aux")
    prefactor = -1.0 / math.sqrt(TRANSFERS * NAUX * OCCUPIED_BANDS)
    screens = [
        from_root(w_screened[0], "ka", q_ids[momentum_transfer])
        for momentum_transfer in range(TRANSFERS)
    ]
    far_cols = jnp.concatenate(
        [
            coefficients[:, :, :OCCUPIED_BANDS],
            coefficients[:, :, band_count : band_count + OCCUPIED_BANDS],
        ],
        axis=2,
    )
    packed = far_cols.reshape(kpoints, orbitals * 2 * OCCUPIED_BANDS // 128, 128)
    spread = lax.all_to_all(packed, "ka", split_axis=1, concat_axis=0, tiled=True)
    permuted = jnp.take(spread, partner, axis=0)
    arrived = jnp.stack(
        [
            lax.all_to_all(
                permuted[momentum_transfer], "ka", split_axis=0, concat_axis=1, tiled=True
            )
            for momentum_transfer in range(TRANSFERS)
        ]
    )
    distant_coefficients = arrived.reshape(
        TRANSFERS, kpoints, CELL_ATOMS, ORBITALS_PER_ATOM, 2 * OCCUPIED_BANDS
    )
    own_rows = lax.dynamic_slice_in_dim(
        coefficients,
        half_index * local_atoms * ORBITALS_PER_ATOM,
        local_atoms * ORBITALS_PER_ATOM,
        1,
    )
    home_coefficients = own_rows.reshape(kpoints, local_atoms, ORBITALS_PER_ATOM, doubled)
    neighbour_coef = jnp.take(distant_coefficients, neighbors, axis=2)
    pair_half = jnp.einsum(
        "tkcjoy,cjox->tkcyx", neighbour_coef, triple, preferred_element_type=jnp.float32
    ).astype(jnp.bfloat16)
    pair_half = pair_half.reshape(
        TRANSFERS, kpoints, local_atoms, 2 * OCCUPIED_BANDS, AUX_ATOM, ORBITALS_PER_ATOM
    )
    combos = jnp.einsum(
        "kcix,tkcyai->tkcayx", home_coefficients, pair_half, preferred_element_type=jnp.float32
    )
    real_part = (
        combos[..., :OCCUPIED_BANDS, :band_count] + combos[..., OCCUPIED_BANDS:, band_count:]
    )
    imag_part = (
        combos[..., OCCUPIED_BANDS:, :band_count] - combos[..., :OCCUPIED_BANDS, band_count:]
    )
    products = jnp.concatenate([real_part, imag_part], axis=-1).astype(jnp.bfloat16)
    products = products.reshape(TRANSFERS, kpoints, local_aux, OCCUPIED_BANDS, doubled)
    pairs = products.reshape(TRANSFERS // 2, 2, kpoints, local_aux, OCCUPIED_BANDS, doubled)
    screen_pairs = jnp.stack(screens).reshape(TRANSFERS // 2, 2, local_aux, 2 * NAUX)
    outgoing = lax.dynamic_index_in_dim(pairs, 1 - half_index, 1, keepdims=False)
    incoming = from_partner(outgoing, "aux", 0)
    own_start = half_index * local_aux
    other_start = (1 - half_index) * local_aux
    full_weights = lax.dynamic_index_in_dim(screen_pairs[0], half_index, 0, keepdims=False)
    part_weights = lax.dynamic_index_in_dim(screen_pairs[0], 1 - half_index, 0, keepdims=False)
    full_values = lax.dynamic_index_in_dim(pairs[0], half_index, 0, keepdims=False)
    part_values = lax.dynamic_index_in_dim(pairs[0], 1 - half_index, 0, keepdims=False)
    cross = apply_block(full_weights, other_start, incoming[0], band_count)
    full_screened = (apply_block(full_weights, own_start, full_values, band_count) + cross).astype(
        jnp.bfloat16
    )
    part_screened = apply_block(part_weights, own_start, part_values, band_count).astype(
        jnp.bfloat16
    )
    cross_screened = cross.astype(jnp.bfloat16)
    diagonal = pair_blocks(full_values, full_screened) + pair_blocks(part_values, part_screened)
    diag_real, diag_imag = sigma_parts(diagonal, band_count)
    cross_real, cross_imag = sigma_parts(pair_blocks(full_values, cross_screened), band_count)
    total_real = diag_real + jnp.transpose(cross_real, (0, 2, 1))
    total_imag = diag_imag - jnp.transpose(cross_imag, (0, 2, 1))
    local_sigma = jnp.concatenate([total_real, total_imag], axis=-1)
    local_sigma = prefactor * local_sigma
    return lax.psum_scatter(
        local_sigma.astype(jnp.bfloat16), "aux", scatter_dimension=1, tiled=True
    ).astype(jnp.float32)


def solution(mesh):
    in_specs = (
        P("ka", None, None),
        P("aux", None, None, None),
        P("aux", None),
        P("ka", "aux", None),
        P(),
        P(),
    )
    out_specs = P("ka", "aux", None)
    return jax.shard_map(local, mesh=mesh, in_specs=in_specs, out_specs=out_specs, check_vma=False)
```

profile of v0, /device:TPU:0, one launch (start us, length us, event | category | flops | bytes accessed | tf_op | source)
XLA Modules:
  0.0 210.7 jit_solution(5651449956877544662)
XLA Ops:
  6.5 2.1 fusion.62
  10.9 2.2 %reduce = bf16[1024,128]{1,0:T(8,128)(2,1)S(1)} reduce(bf16[1024,1,128]{2,1,0:T(2,128)(2,1)S(1)} %bitcast.159, bf16[]{:T(256)} %broadcast.52), dimensions={1}, to_apply=%bitcast.134.reduce_sub_computation | reduce | bytes 524290
  13.9 7.4 %all-to-all-start = ((bf16[16,2,4096]{2,1,0:T(2,128)(2,1)}), bf16[16,2,4096]{2,1,0:T(2,128)(2,1)S(1)}, u32[]{:S(2)}, u32[]{:S(2)}) async-start(bf16[16,2,4096]{2,1,0:T(2,128)(2,1)} %reshape.297), calls=%async_computation | async-start | bytes 524288 | tf_op jit(solution)/shard_map/all_to_all | solution.py:76
  23.3 8.0 %all-to-all-done = bf16[16,2,4096]{2,1,0:T(2,128)(2,1)S(1)} async-done(((bf16[16,2,4096]{2,1,0:T(2,128)(2,1)}), bf16[16,2,4096]{2,1,0:T(2,128)(2,1)S(1)}, u32[]{:S(2)}, u32[]{:S(2)}) %all-to-all-start) | async-done | bytes 262176 | tf_op jit(solution)/shard_map/all_to_all | solution.py:76
  33.3 3.5 %all-to-all-start.1 = ((bf16[16,64,128]{2,1,0:T(8,128)(2,1)}), bf16[16,64,128]{2,1,0:T(8,128)(2,1)S(1)}, u32[]{:S(2)}, u32[]{:S(2)}) async-start(bf16[16,64,128]{2,1,0:T(8,128)(2,1)} %get-tuple-element.21), calls=%async_computation.1 | async-start | bytes 524288 | tf_op jit(solution)/shard_map/all_to_all | solution.py:80
  39.3 7.4 %all-to-all-done.1 = bf16[16,64,128]{2,1,0:T(8,128)(2,1)S(1)} async-done(((bf16[16,64,128]{2,1,0:T(8,128)(2,1)}), bf16[16,64,128]{2,1,0:T(8,128)(2,1)S(1)}, u32[]{:S(2)}, u32[]{:S(2)}) %all-to-all-start.1) | async-done | bytes 262176 | tf_op jit(solution)/shard_map/all_to_all | solution.py:80
  46.8 3.5 %all-to-all-start.2 = ((bf16[16,64,128]{2,1,0:T(8,128)(2,1)}), bf16[16,64,128]{2,1,0:T(8,128)(2,1)S(1)}, u32[]{:S(2)}, u32[]{:S(2)}) async-start(bf16[16,64,128]{2,1,0:T(8,128)(2,1)} %get-tuple-element.22), calls=%async_computation.2 | async-start | bytes 524288 | tf_op jit(solution)/shard_map/all_to_all | solution.py:80
  52.0 11.2 %all-to-all-done.2 = bf16[16,64,128]{2,1,0:T(8,128)(2,1)S(1)} async-done(((bf16[16,64,128]{2,1,0:T(8,128)(2,1)}), bf16[16,64,128]{2,1,0:T(8,128)(2,1)S(1)}, u32[]{:S(2)}, u32[]{:S(2)}) %all-to-all-start.2) | async-done | bytes 262176 | tf_op jit(solution)/shard_map/all_to_all | solution.py:80
  66.2 2.1 %gather_fusion.1 = bf16[64,2,64,32]{3,2,1,0:T(8,128)(2,1)} fusion(bf16[2,64,64,32]{3,2,1,0:T(8,128)(2,1)S(1)} %maximum_bitcast_fusion, s32[1024]{0:T(1024)S(1)} %pad_clamp_fusion), kind=kCustom, calls=%fused_computation.1 | custom fusion | bytes 1048832 | tf_op jit(solution)/shard_map/jit(_take)/gather | solution.py:96
  68.4 2.8 %copy.46 = bf16[64,2,64,32]{2,3,1,0:T(8,128)(2,1)} copy(bf16[64,2,64,32]{3,2,1,0:T(8,128)(2,1)} %gather_fusion.1) | data formatting | bytes 1048576 | tf_op jit(solution)/shard_map/jit(_take)/gather | solution.py:96
  71.1 4.9 %fusion.9 = bf16[2,1,32,32,768]{4,3,0,2,1:T(8,128)(2,1)S(1)} fusion(bf16[32,2,64,768]{3,2,1,0:T(8,128)(2,1)} %param.7, bf16[32,2,2,64,32]{3,4,2,1,0:T(8,128)(2,1)} %bitcast.155, pred[32,2]{1,0:T(8,128)(4,1)S(1)} %copy.40), kind=kOutput, calls=%fused_computation.12 | convolution fusion | flops 404488192 | bytes 9961536 | tf_op jit(solution)/shard_map/tkcjoy,cjox->tkcyx/dot_general | solution.py:97
  76.0 7.2 %reshape.296 = bf16[2,32,32,12,64]{4,3,2,0,1:T(8,128)(2,1)} reshape(bf16[2,1,32,32,768]{4,3,0,2,1:T(8,128)(2,1)S(1)} %fusion.9) | data formatting | bytes 6291456 | tf_op jit(solution)/shard_map/reshape.12
  83.2 5.1 %fusion.6 = f32[2,1,32,12,32,128]{5,4,3,0,2,1:T(8,128)S(1)} fusion(bf16[32,64,128,1,1]{2,1,4,3,0:T(8,128)(2,1)} %bitcast.160, bf16[2,32,32,12,64]{4,3,2,0,1:T(8,128)(2,1)} %reshape.296), kind=kOutput, calls=%fused_computation.11 | convolution fusion | flops 402653184 | bytes 16252928 | tf_op jit(solution)/shard_map/kcix,tkcyai->tkcayx/dot_general | solution.py:103
  88.3 3.7 %fusion = (bf16[2,1,32,12,16,64]{5,4,3,0,2,1:T(8,128)(2,1)S(1)}, bf16[2,1,32,12,16,64]{5,4,3,0,2,1:T(8,128)(2,1)S(1)}) fusion(f32[2,1,32,12,32,128]{5,4,3,0,2,1:T(8,128)S(1)} %fusion.6), kind=kLoop, calls=%fused_computation.3 | loop fusion | flops 3145728 | bytes 15728640 | tf_op jit(solution)/shard_map/convert.6
  93.3 2.1 fusion.17
  99.3 2.0 pad_maximum_fusion.2
  102.0 2.1 %pad_maximum_fusion = bf16[1,384,16,128]{3,2,1,0:T(8,128)(2,1)} fusion(bf16[1,384,16,64]{3,2,1,0:T(8,128)(2,1)S(1)} %get-tuple-element.14, bf16[1,384,16,64]{3,2,1,0:T(8,128)(2,1)S(1)} %get-tuple-element.13), kind=kLoop, calls=%fused_computation.47 | loop fusion | flops 3145728 | bytes 3145728 | tf_op jit(solution)/shard_map/concatenate | solution.py:27
  104.1 42.1 %all-reduce.3.cloned.1.call-done = (bf16[1,384,1536]{2,1,0:T(8,128)(2,1)}, bf16[1,384,1536]{2,1,0:T(8,128)(2,1)}) async-done(((bf16[1,384,1536]{2,1,0:T(8,128)(2,1)}, bf16[1,384,1536]{2,1,0:T(8,128)(2,1)}), (bf16[1,384,1536]{2,1,0:T(8,128)(2,1)}, bf16[1,384,1536]{2,1,0:T(8,128)(2,1)})) %all-reduce.3.cloned.1.call-update) | async-done | bytes 2359312 | tf_op jit(solution)/shard_map/psum | solution.py:17
  150.2 2.5 %fusion.11 = bf16[1,384,2048]{1,2,0:T(8,128)(2,1)} fusion(f32[2048,384]{1,0:T(8,128)S(1)} %fusion.20, bf16[48,8,16,128]{3,2,1,0:T(8,128)(2,1)S(1)} %bitcast.157, bf16[2,384,1536]{2,1,0:T(8,128)(2,1)S(1)} %constant_dynamic-update-slice_fusion, s32[]{:T(128)S(6)} %select_n.104, s32[]{:T(128)S(6)} %select_n.98), kind=kOutput, calls=%fused_computation.23 | convolution fusion | flops 605552640 | bytes 6586376 | tf_op jit(solution)/shard_map/ab,kbx->kax/dot_general | solution.py:37
  152.7 2.6 %copy.55 = bf16[1,384,2048]{2,1,0:T(8,128)(2,1)} copy(bf16[1,384,2048]{1,2,0:T(8,128)(2,1)} %fusion.11) | data formatting | bytes 3145728 | tf_op jit(solution)/shard_map/convert_element_type | solution.py:128
  155.3 3.7 %convert_element_type.101 = bf16[6144,128]{1,0:T(8,128)(2,1)} reshape(bf16[1,384,2048]{2,1,0:T(8,128)(2,1)} %copy.55) | data formatting | bytes 3145728 | tf_op jit(solution)/shard_map/convert_element_type | solution.py:128
  159.1 2.3 %fusion.30 = f32[2048,384]{1,0:T(8,128)S(1)} fusion(bf16[48,8,16,128]{3,2,1,0:T(8,128)(2,1)S(1)} %bitcast.144, bf16[2,384,1536]{2,1,0:T(8,128)(2,1)} %copy-done.5, s32[]{:T(128)S(6)} %select_n.94, s32[]{:T(128)S(6)} %select_n.96), kind=kOutput, calls=%fused_computation.41 | convolution fusion | flops 603979776 | bytes 5013512 | tf_op jit(solution)/shard_map/ab,kbx->kax/dot_general | solution.py:36
  161.3 2.6 %slice_negate_fusion.1 = (bf16[1,384,16,64]{3,2,1,0:T(8,128)(2,1)S(1)}, bf16[1,384,16,64]{3,2,1,0:T(8,128)(2,1)S(1)}) fusion(bf16[1,384,16,128]{3,2,1,0:T(8,128)(2,1)} %bitcast.31), kind=kLoop, calls=%fused_computation.45 | loop fusion | flops 393216 | bytes 3145728 | tf_op jit(solution)/shard_map/neg | solution.py:27
  164.8 2.2 %fusion.23 = f32[2048,384]{1,0:T(8,128)S(1)} fusion(bf16[48,8,16,128]{3,2,1,0:T(8,128)(2,1)S(1)} %bitcast.154, bf16[2,384,1536]{2,1,0:T(8,128)(2,1)} %copy-done.5, s32[]{:T(128)S(6)} %select_n.94, s32[]{:T(128)S(6)} %select_n.103), kind=kOutput, calls=%fused_computation.34 | convolution fusion | flops 603979776 | bytes 5013512 | tf_op jit(solution)/shard_map/ab,kbx->kax/dot_general | solution.py:37
  167.0 2.8 %convolution_add_fusion = f32[2048,384]{1,0:T(8,128)S(1)} fusion(f32[2048,384]{1,0:T(8,128)S(1)} %fusion.23, bf16[48,8,16,128]{3,2,1,0:T(8,128)(2,1)} %bitcast.70, bf16[2,384,1536]{2,1,0:T(8,128)(2,1)} %copy-done.5, s32[]{:T(128)S(6)} %select_n.94, s32[]{:T(128)S(6)} %select_n.101), kind=kOutput, calls=%fused_computation.17 | convolution fusion | flops 604766208 | bytes 8159240 | tf_op jit(solution)/shard_map/ab,kbx->kax/dot_general | solution.py:36
  171.8 3.6 %fusion.10 = bf16[1,384,2048]{1,2,0:T(8,128)(2,1)} fusion(f32[2048,384]{1,0:T(8,128)S(1)} %convolution_add_fusion, f32[2048,384]{1,0:T(8,128)S(1)} %fusion.30, bf16[48,8,16,128]{3,2,1,0:T(8,128)(2,1)S(1)} %bitcast.156, bf16[2,384,1536]{2,1,0:T(8,128)(2,1)} %copy-done.5, s32[]{:T(128)S(6)} %select_n.94, s32[]{:T(128)S(6)} %select_n.98), kind=kOutput, calls=%fused_computation.22 | convolution fusion | flops 606339072 | bytes 9732104 | tf_op jit(solution)/shard_map/ab,kbx->kax/dot_general | solution.py:37
  175.4 2.7 %copy.54 = bf16[1,384,2048]{2,1,0:T(8,128)(2,1)} copy(bf16[1,384,2048]{1,2,0:T(8,128)(2,1)} %fusion.10) | data formatting | bytes 3145728 | tf_op jit(solution)/shard_map/convert_element_type | solution.py:125
  178.1 3.7 %convert_element_type.97 = bf16[6144,128]{1,0:T(8,128)(2,1)} reshape(bf16[1,384,2048]{2,1,0:T(8,128)(2,1)} %copy.54) | data formatting | bytes 3145728 | tf_op jit(solution)/shard_map/convert_element_type | solution.py:125
  181.8 2.6 %copy.56 = bf16[1,384,2048]{2,1,0:T(8,128)(2,1)} copy(bf16[1,384,2048]{1,2,0:T(8,128)(2,1)} %convert_bitcast_fusion) | data formatting | bytes 3145728 | tf_op jit(solution)/shard_map/convert_element_type | solution.py:131
  184.4 3.7 %convert_element_type.105 = bf16[6144,128]{1,0:T(8,128)(2,1)} reshape(bf16[1,384,2048]{2,1,0:T(8,128)(2,1)} %copy.56) | data formatting | bytes 3145728 | tf_op jit(solution)/shard_map/convert_element_type | solution.py:131
  188.2 2.1 %fusion.64 = f32[128,128]{1,0:T(8,128)S(1)} fusion(bf16[6144,128]{1,0:T(8,128)(2,1)S(1)} %bitcast.145, bf16[6144,128]{1,0:T(8,128)(2,1)} %convert_element_type.97), kind=kOutput, calls=%fused_computation.104 | convolution fusion | flops 201326592 | bytes 3211264 | tf_op jit(solution)/shard_map/kxm,kxn->kmn/dot_general | solution.py:48
  193.2 9.4 %reduce-scatter.2.cloned.1.call-done = bf16[1,32,128]{2,1,0:T(8,128)(2,1)} async-done(((bf16[1,64,128]{2,1,0:T(8,128)(2,1)}), bf16[1,32,128]{2,1,0:T(8,128)(2,1)}) %reduce-scatter.2.cloned.1.call-update) | async-done | bytes 8208 | tf_op jit(solution)/shard_map/reduce_scatter | solution.py:139
  (71 shorter events, 29.6 us)
Async XLA Ops:
  9.7 11.6 %copy-start.9 = (s32[2,16]{1,0:T(2,128)S(1)}, s32[2,16]{1,0:T(2,128)}, u32[]{:S(2)}) copy-start(s32[2,16]{1,0:T(2,128)} %param.10) | copy-start | bytes 388
  9.8 11.7 %copy-start.8 = (s32[2]{0:T(128)S(1)}, s32[2]{0:T(128)}, u32[]{:S(2)}) copy-start(s32[2]{0:T(128)} %param.11) | copy-start | bytes 28
  13.9 17.4 %all-to-all-start = ((bf16[16,2,4096]{2,1,0:T(2,128)(2,1)}), bf16[16,2,4096]{2,1,0:T(2,128)(2,1)S(1)}, u32[]{:S(2)}, u32[]{:S(2)}) async-start(bf16[16,2,4096]{2,1,0:T(2,128)(2,1)} %reshape.297), calls=%async_computation | async-start | bytes 524288 | tf_op jit(solution)/shard_map/all_to_all | solution.py:76
  32.3 4.6 %copy-start.7 = (bf16[1,384,1536]{2,1,0:T(8,128)(2,1)S(1)}, bf16[1,384,1536]{2,1,0:T(8,128)(2,1)}, u32[]{:S(2)}) copy-start(bf16[1,384,1536]{2,1,0:T(8,128)(2,1)} %param.9) | copy-start | bytes 3538948
  33.3 13.5 %all-to-all-start.1 = ((bf16[16,64,128]{2,1,0:T(8,128)(2,1)}), bf16[16,64,128]{2,1,0:T(8,128)(2,1)S(1)}, u32[]{:S(2)}, u32[]{:S(2)}) async-start(bf16[16,64,128]{2,1,0:T(8,128)(2,1)} %get-tuple-element.21), calls=%async_computation.1 | async-start | bytes 524288 | tf_op jit(solution)/shard_map/all_to_all | solution.py:80
  36.8 109.4 %all-reduce.3.cloned.1.call-start = ((), (), s32[]{:S(2)}) async-start(), calls=%async_computation.5 | async-start | bytes 4718592 | tf_op jit(solution)/shard_map/psum | solution.py:17
  38.5 0.7 copy-start.10
  38.5 12.2 %copy-start = (bf16[1,4096,128]{2,1,0:T(8,128)(2,1)S(1)}, bf16[1,4096,128]{2,1,0:T(8,128)(2,1)}, u32[]{:S(2)}) copy-start(bf16[1,4096,128]{2,1,0:T(8,128)(2,1)} %param.6) | copy-start | bytes 3145732
  46.8 16.4 %all-to-all-start.2 = ((bf16[16,64,128]{2,1,0:T(8,128)(2,1)}), bf16[16,64,128]{2,1,0:T(8,128)(2,1)S(1)}, u32[]{:S(2)}, u32[]{:S(2)}) async-start(bf16[16,64,128]{2,1,0:T(8,128)(2,1)} %get-tuple-element.22), calls=%async_computation.2 | async-start | bytes 524288 | tf_op jit(solution)/shard_map/all_to_all | solution.py:80
  50.3 152.2 %reduce-scatter.2.cloned.1.call-start = ((), (), s32[]{:S(2)}) async-start(), calls=%async_computation.4 | async-start | bytes 24576 | tf_op jit(solution)/shard_map/reduce_scatter | solution.py:139
  95.4 65.9 %collective-permute-start = (bf16[1,1,384,16,128]{4,3,2,1,0:T(8,128)(2,1)}, bf16[1,1,384,16,128]{4,3,2,1,0:T(8,128)(2,1)}, u32[]{:S(2)}, u32[]{:S(2)}) collective-permute-start(bf16[1,1,384,16,128]{4,3,2,1,0:T(8,128)(2,1)} %fusion.17), channel_id=1, source_target_pairs={{0,1},{1,0},{2,3},{3,2},{4,5},{5,4},{6,7},{7,6},{8,9},{9,8},{10,11... | collective-permute-start | bytes 4718600 | tf_op jit(solution)/shard_map/ppermute | solution.py:23
  146.2 1.6 copy-start.6
  147.9 1.4 copy-start.5
  147.9 2.3 %copy-start.4 = (bf16[1,384,16,128]{3,2,1,0:T(8,128)(2,1)S(1)}, bf16[1,384,16,128]{3,2,1,0:T(8,128)(2,1)}, u32[]{:S(2)}) copy-start(bf16[1,384,16,128]{3,2,1,0:T(8,128)(2,1)} %pad_maximum_fusion.2) | copy-start | bytes 4718596
  169.8 2.0 copy-start.1
  188.2 2.1 %copy-start.3 = (bf16[6144,128]{1,0:T(8,128)(2,1)S(1)}, bf16[6144,128]{1,0:T(8,128)(2,1)}, u32[]{:S(2)}) copy-start(bf16[6144,128]{1,0:T(8,128)(2,1)} %convert_element_type.105) | copy-start | bytes 4718596
  190.3 1.4 copy-start.2
Sparse Core Ops, SparseCore 0:
  41.2 104.9 all-reduce.2
  193.3 9.2 reduce-scatter.1
where the time goes:
time: 212 us; the launch traced here: 211 us
  waiting for transfers between devices  78.2 us (37%)
  local copies, waits for them, and re-layouts  47.6 us (22%)
  matrix products  28.1 us (13%)
  other arithmetic  25.5 us (12%)
  starting transfers between devices  16.3 us (8%)
  between operations  15.1 us (7%)
    psum x1, waiting for transfers between devices, from_root(): return lax.psum(block, axis)  42.1 us
    all_to_all x2, waiting for transfers between devices, local(): lax.all_to_all(permuted[momentum_transfer], 'ka', split_axis=0, concat_ax...  18.6 us
    reduce_scatter x1, waiting for transfers between devices, local(): lax.psum_scatter(local_sigma.astype(jnp.bfloat16), 'aux', scatter_dimensi...  9.4 us
    another operation x3, local copies, waits for them, and re-layouts  8.42 us
    dot_general x3, matrix products, apply_block(): jnp.einsum('ab,kbx->kax', imag_cols, turned, preferred_element_type=jnp.f...  8.36 us
    all_to_all x1, waiting for transfers between devices, local(): lax.all_to_all(packed, 'ka', split_axis=1, concat_axis=0, tiled=True)  8.01 us
    all_to_all x1, starting transfers between devices, local(): lax.all_to_all(packed, 'ka', split_axis=1, concat_axis=0, tiled=True)  7.41 us
    all_to_all x2, starting transfers between devices, local(): lax.all_to_all(permuted[momentum_transfer], 'ka', split_axis=0, concat_ax...  7.06 us
  transfers between devices with their start and end apart: 6, of which 5 were waited for; matrix products, arithmetic and copies ran while one was open for 27% of the time, Pallas kernels for 0%

commit v1 on v0

--- a/solution.py
+++ b/solution.py
@@ -77,8 +77,14 @@
     permuted = jnp.take(spread, partner, axis=0)
     arrived = jnp.stack(
         [
-            lax.all_to_all(
-                permuted[momentum_transfer], "ka", split_axis=0, concat_axis=1, tiled=True
+            jnp.concatenate(
+                lax.all_to_all(
+                    jnp.stack(jnp.split(permuted[momentum_transfer], lax.axis_size("ka"), axis=0)),
+                    "ka",
+                    0,
+                    0,
+                ),
+                axis=1,
             )
             for momentum_transfer in range(TRANSFERS)
         ]

time: 212 us -> 221 us (1.042)
  local copies, waits for them, and re-layouts: 47.6 us -> 56.6 us
    unnamed x29 -> x44, local copies, waits for them, and re-layouts: 6.87 us -> 16 us
    another operation x5 -> x6, local copies, waits for them, and re-layouts: 10.2 us -> 10.9 us
  transfers between devices with their start and end apart: 6 -> 6, of which waited for: 5 -> 5; matrix products, arithmetic and copies ran while one was open for 27% -> 26% of each run, Pallas kernels for 0% -> 0%
where the time goes in v1:
time: 221 us; the launch traced here: 220 us
  waiting for transfers between devices  78.1 us (35%)
  local copies, waits for them, and re-layouts  56.6 us (26%)
  matrix products  28 us (13%)
  other arithmetic  25.6 us (12%)
  starting transfers between devices  16.3 us (7%)
  between operations  15.1 us (7%)
    psum x1, waiting for transfers between devices, from_root(): return lax.psum(block, axis)  42.1 us
    all_to_all x2, waiting for transfers between devices, local(): lax.all_to_all(jnp.stack(jnp.split(permuted[momentum_transfer], lax.axis_...  18.5 us
    unnamed x44, local copies, waits for them, and re-layouts  16 us
    reduce_scatter x1, waiting for transfers between devices, local(): lax.psum_scatter(local_sigma.astype(jnp.bfloat16), 'aux', scatter_dimensi...  9.4 us
    another operation x3, local copies, waits for them, and re-layouts  8.44 us
    dot_general x3, matrix products, apply_block(): jnp.einsum('ab,kbx->kax', imag_cols, turned, preferred_element_type=jnp.f...  8.31 us
    all_to_all x1, waiting for transfers between devices, local(): lax.all_to_all(packed, 'ka', split_axis=1, concat_axis=0, tiled=True)  8 us
    all_to_all x1, starting transfers between devices, local(): lax.all_to_all(packed, 'ka', split_axis=1, concat_axis=0, tiled=True)  7.41 us
  transfers between devices with their start and end apart: 6, of which 5 were waited for; matrix products, arithmetic and copies ran while one was open for 26% of the time, Pallas kernels for 0%

profile of v1, /device:TPU:0, one launch (start us, length us, event | category | flops | bytes accessed | tf_op | source)
XLA Modules:
  0.0 219.8 jit_solution(2579364950900360831)
XLA Ops:
  6.5 2.1 fusion.62
  10.9 2.2 %reduce = bf16[1024,128]{1,0:T(8,128)(2,1)S(1)} reduce(bf16[1024,1,128]{2,1,0:T(2,128)(2,1)S(1)} %bitcast.159, bf16[]{:T(256)} %broadcast.52), dimensions={1}, to_apply=%bitcast.134.reduce_sub_computation | reduce | bytes 524290
  13.9 7.4 %all-to-all-start = ((bf16[16,2,4096]{2,1,0:T(2,128)(2,1)}), bf16[16,2,4096]{2,1,0:T(2,128)(2,1)S(1)}, u32[]{:S(2)}, u32[]{:S(2)}) async-start(bf16[16,2,4096]{2,1,0:T(2,128)(2,1)} %reshape.353), calls=%async_computation | async-start | bytes 524288 | tf_op jit(solution)/shard_map/all_to_all | solution.py:76
  23.3 8.0 %all-to-all-done = bf16[16,2,4096]{2,1,0:T(2,128)(2,1)S(1)} async-done(((bf16[16,2,4096]{2,1,0:T(2,128)(2,1)}), bf16[16,2,4096]{2,1,0:T(2,128)(2,1)S(1)}, u32[]{:S(2)}, u32[]{:S(2)}) %all-to-all-start) | async-done | bytes 262176 | tf_op jit(solution)/shard_map/all_to_all | solution.py:76
  42.2 3.5 %all-to-all-start.1 = ((bf16[16,1,64,128]{3,2,1,0:T(8,128)(2,1)}), bf16[16,1,64,128]{3,2,1,0:T(8,128)(2,1)S(1)}, u32[]{:S(2)}, u32[]{:S(2)}) async-start(bf16[16,1,64,128]{3,2,1,0:T(8,128)(2,1)} %get-tuple-element.21), calls=%async_computation.1 | async-start | bytes 524288 | tf_op jit(solution)/shard_map/all_to_all | solution.py:81
  48.4 7.4 %all-to-all-done.1 = bf16[16,1,64,128]{3,2,1,0:T(8,128)(2,1)S(1)} async-done(((bf16[16,1,64,128]{3,2,1,0:T(8,128)(2,1)}), bf16[16,1,64,128]{3,2,1,0:T(8,128)(2,1)S(1)}, u32[]{:S(2)}, u32[]{:S(2)}) %all-to-all-start.1) | async-done | bytes 262176 | tf_op jit(solution)/shard_map/all_to_all | solution.py:81
  55.7 3.5 %all-to-all-start.2 = ((bf16[16,1,64,128]{3,2,1,0:T(8,128)(2,1)}), bf16[16,1,64,128]{3,2,1,0:T(8,128)(2,1)S(1)}, u32[]{:S(2)}, u32[]{:S(2)}) async-start(bf16[16,1,64,128]{3,2,1,0:T(8,128)(2,1)} %get-tuple-element.22), calls=%async_computation.2 | async-start | bytes 524288 | tf_op jit(solution)/shard_map/all_to_all | solution.py:81
  60.9 11.2 %all-to-all-done.2 = bf16[16,1,64,128]{3,2,1,0:T(8,128)(2,1)S(1)} async-done(((bf16[16,1,64,128]{3,2,1,0:T(8,128)(2,1)}), bf16[16,1,64,128]{3,2,1,0:T(8,128)(2,1)S(1)}, u32[]{:S(2)}, u32[]{:S(2)}) %all-to-all-start.2) | async-done | bytes 262176 | tf_op jit(solution)/shard_map/all_to_all | solution.py:81
  75.2 2.2 gather_fusion.1
  77.4 2.7 %copy.60 = bf16[64,2,64,32]{2,3,1,0:T(8,128)(2,1)} copy(bf16[64,2,64,32]{3,2,1,0:T(8,128)(2,1)} %gather_fusion.1) | data formatting | bytes 1048576 | tf_op jit(solution)/shard_map/jit(_take)/gather | solution.py:102
  80.1 4.9 %fusion.9 = bf16[2,1,32,32,768]{4,3,0,2,1:T(8,128)(2,1)S(1)} fusion(bf16[32,2,64,768]{3,2,1,0:T(8,128)(2,1)} %param.7, bf16[32,2,2,64,32]{3,4,2,1,0:T(8,128)(2,1)} %bitcast.155, pred[32,2]{1,0:T(8,128)(4,1)S(1)} %copy.54), kind=kOutput, calls=%fused_computation.12 | convolution fusion | flops 404488192 | bytes 9961536 | tf_op jit(solution)/shard_map/tkcjoy,cjox->tkcyx/dot_general | solution.py:103
  85.0 7.2 %reshape.352 = bf16[2,32,32,12,64]{4,3,2,0,1:T(8,128)(2,1)} reshape(bf16[2,1,32,32,768]{4,3,0,2,1:T(8,128)(2,1)S(1)} %fusion.9) | data formatting | bytes 6291456 | tf_op jit(solution)/shard_map/reshape.88
  92.2 5.1 %fusion.6 = f32[2,1,32,12,32,128]{5,4,3,0,2,1:T(8,128)S(1)} fusion(bf16[32,64,128,1,1]{2,1,4,3,0:T(8,128)(2,1)} %bitcast.160, bf16[2,32,32,12,64]{4,3,2,0,1:T(8,128)(2,1)} %reshape.352), kind=kOutput, calls=%fused_computation.11 | convolution fusion | flops 402653184 | bytes 16252928 | tf_op jit(solution)/shard_map/kcix,tkcyai->tkcayx/dot_general | solution.py:109
  97.3 3.7 %fusion = (bf16[2,1,32,12,16,64]{5,4,3,0,2,1:T(8,128)(2,1)S(1)}, bf16[2,1,32,12,16,64]{5,4,3,0,2,1:T(8,128)(2,1)S(1)}) fusion(f32[2,1,32,12,32,128]{5,4,3,0,2,1:T(8,128)S(1)} %fusion.6), kind=kLoop, calls=%fused_computation.3 | loop fusion | flops 3145728 | bytes 15728640 | tf_op jit(solution)/shard_map/convert.6
  102.3 2.1 fusion.17
  108.3 2.0 pad_maximum_fusion.2
  111.0 2.1 pad_maximum_fusion
  113.0 42.1 %all-reduce.3.cloned.1.call-done = (bf16[1,384,1536]{2,1,0:T(8,128)(2,1)}, bf16[1,384,1536]{2,1,0:T(8,128)(2,1)}) async-done(((bf16[1,384,1536]{2,1,0:T(8,128)(2,1)}, bf16[1,384,1536]{2,1,0:T(8,128)(2,1)}), (bf16[1,384,1536]{2,1,0:T(8,128)(2,1)}, bf16[1,384,1536]{2,1,0:T(8,128)(2,1)})) %all-reduce.3.cloned.1.call-update) | async-done | bytes 2359312 | tf_op jit(solution)/shard_map/psum | solution.py:17
  159.2 2.5 %fusion.11 = bf16[1,384,2048]{1,2,0:T(8,128)(2,1)} fusion(f32[2048,384]{1,0:T(8,128)S(1)} %fusion.20, bf16[48,8,16,128]{3,2,1,0:T(8,128)(2,1)S(1)} %bitcast.157, bf16[2,384,1536]{2,1,0:T(8,128)(2,1)S(1)} %constant_dynamic-update-slice_fusion.32, s32[]{:T(128)S(6)} %select_n.104, s32[]{:T(128)S(6)} %select_n.98), kind=kOutput, calls=%fused_computation.23 | convolution fusion | flops 605552640 | bytes 6586376 | tf_op jit(solution)/shard_map/ab,kbx->kax/dot_general | solution.py:37
  161.6 2.6 %copy.69 = bf16[1,384,2048]{2,1,0:T(8,128)(2,1)} copy(bf16[1,384,2048]{1,2,0:T(8,128)(2,1)} %fusion.11) | data formatting | bytes 3145728 | tf_op jit(solution)/shard_map/convert_element_type | solution.py:134
  164.3 3.7 %convert_element_type.101 = bf16[6144,128]{1,0:T(8,128)(2,1)} reshape(bf16[1,384,2048]{2,1,0:T(8,128)(2,1)} %copy.69) | data formatting | bytes 3145728 | tf_op jit(solution)/shard_map/convert_element_type | solution.py:134
  168.0 2.3 %fusion.30 = f32[2048,384]{1,0:T(8,128)S(1)} fusion(bf16[48,8,16,128]{3,2,1,0:T(8,128)(2,1)S(1)} %bitcast.144, bf16[2,384,1536]{2,1,0:T(8,128)(2,1)} %copy-done.5, s32[]{:T(128)S(6)} %select_n.94, s32[]{:T(128)S(6)} %select_n.96), kind=kOutput, calls=%fused_computation.41 | convolution fusion | flops 603979776 | bytes 5013512 | tf_op jit(solution)/shard_map/ab,kbx->kax/dot_general | solution.py:36
  170.3 2.7 %slice_negate_fusion.1 = (bf16[1,384,16,64]{3,2,1,0:T(8,128)(2,1)S(1)}, bf16[1,384,16,64]{3,2,1,0:T(8,128)(2,1)S(1)}) fusion(bf16[1,384,16,128]{3,2,1,0:T(8,128)(2,1)} %bitcast.29), kind=kLoop, calls=%fused_computation.45 | loop fusion | flops 393216 | bytes 3145728 | tf_op jit(solution)/shard_map/neg | solution.py:27
  173.8 2.2 %fusion.23 = f32[2048,384]{1,0:T(8,128)S(1)} fusion(bf16[48,8,16,128]{3,2,1,0:T(8,128)(2,1)S(1)} %bitcast.154, bf16[2,384,1536]{2,1,0:T(8,128)(2,1)} %copy-done.5, s32[]{:T(128)S(6)} %select_n.94, s32[]{:T(128)S(6)} %select_n.103), kind=kOutput, calls=%fused_computation.34 | convolution fusion | flops 603979776 | bytes 5013512 | tf_op jit(solution)/shard_map/ab,kbx->kax/dot_general | solution.py:37
  176.0 2.8 %convolution_add_fusion = f32[2048,384]{1,0:T(8,128)S(1)} fusion(f32[2048,384]{1,0:T(8,128)S(1)} %fusion.23, bf16[48,8,16,128]{3,2,1,0:T(8,128)(2,1)} %bitcast.70, bf16[2,384,1536]{2,1,0:T(8,128)(2,1)} %copy-done.5, s32[]{:T(128)S(6)} %select_n.94, s32[]{:T(128)S(6)} %select_n.101), kind=kOutput, calls=%fused_computation.17 | convolution fusion | flops 604766208 | bytes 8159240 | tf_op jit(solution)/shard_map/ab,kbx->kax/dot_general | solution.py:36
  180.8 3.6 %fusion.10 = bf16[1,384,2048]{1,2,0:T(8,128)(2,1)} fusion(f32[2048,384]{1,0:T(8,128)S(1)} %convolution_add_fusion, f32[2048,384]{1,0:T(8,128)S(1)} %fusion.30, bf16[48,8,16,128]{3,2,1,0:T(8,128)(2,1)S(1)} %bitcast.156, bf16[2,384,1536]{2,1,0:T(8,128)(2,1)} %copy-done.5, s32[]{:T(128)S(6)} %select_n.94, s32[]{:T(128)S(6)} %select_n.98), kind=kOutput, calls=%fused_computation.22 | convolution fusion | flops 606339072 | bytes 9732104 | tf_op jit(solution)/shard_map/ab,kbx->kax/dot_general | solution.py:37
  184.4 2.7 %copy.68 = bf16[1,384,2048]{2,1,0:T(8,128)(2,1)} copy(bf16[1,384,2048]{1,2,0:T(8,128)(2,1)} %fusion.10) | data formatting | bytes 3145728 | tf_op jit(solution)/shard_map/convert_element_type | solution.py:131
  187.1 3.7 %convert_element_type.97 = bf16[6144,128]{1,0:T(8,128)(2,1)} reshape(bf16[1,384,2048]{2,1,0:T(8,128)(2,1)} %copy.68) | data formatting | bytes 3145728 | tf_op jit(solution)/shard_map/convert_element_type | solution.py:131
  190.8 2.6 %copy.70 = bf16[1,384,2048]{2,1,0:T(8,128)(2,1)} copy(bf16[1,384,2048]{1,2,0:T(8,128)(2,1)} %convert_bitcast_fusion) | data formatting | bytes 3145728 | tf_op jit(solution)/shard_map/convert_element_type | solution.py:137
  193.4 3.8 %convert_element_type.105 = bf16[6144,128]{1,0:T(8,128)(2,1)} reshape(bf16[1,384,2048]{2,1,0:T(8,128)(2,1)} %copy.70) | data formatting | bytes 3145728 | tf_op jit(solution)/shard_map/convert_element_type | solution.py:137
  197.2 2.1 fusion.64
  202.2 9.4 %reduce-scatter.2.cloned.1.call-done = bf16[1,32,128]{2,1,0:T(8,128)(2,1)} async-done(((bf16[1,64,128]{2,1,0:T(8,128)(2,1)}), bf16[1,32,128]{2,1,0:T(8,128)(2,1)}) %reduce-scatter.2.cloned.1.call-update) | async-done | bytes 8208 | tf_op jit(solution)/shard_map/reduce_scatter | solution.py:145
  (86 shorter events, 38.6 us)
Async XLA Ops:
  9.7 11.6 %copy-start.9 = (s32[2,16]{1,0:T(2,128)S(1)}, s32[2,16]{1,0:T(2,128)}, u32[]{:S(2)}) copy-start(s32[2,16]{1,0:T(2,128)} %param.10) | copy-start | bytes 388
  9.8 11.7 %copy-start.8 = (s32[2]{0:T(128)S(1)}, s32[2]{0:T(128)}, u32[]{:S(2)}) copy-start(s32[2]{0:T(128)} %param.11) | copy-start | bytes 28
  13.9 17.4 %all-to-all-start = ((bf16[16,2,4096]{2,1,0:T(2,128)(2,1)}), bf16[16,2,4096]{2,1,0:T(2,128)(2,1)S(1)}, u32[]{:S(2)}, u32[]{:S(2)}) async-start(bf16[16,2,4096]{2,1,0:T(2,128)(2,1)} %reshape.353), calls=%async_computation | async-start | bytes 524288 | tf_op jit(solution)/shard_map/all_to_all | solution.py:76
  32.3 13.5 %copy-start.7 = (bf16[1,384,1536]{2,1,0:T(8,128)(2,1)S(1)}, bf16[1,384,1536]{2,1,0:T(8,128)(2,1)}, u32[]{:S(2)}) copy-start(bf16[1,384,1536]{2,1,0:T(8,128)(2,1)} %param.9) | copy-start | bytes 3538948
  42.2 13.5 %all-to-all-start.1 = ((bf16[16,1,64,128]{3,2,1,0:T(8,128)(2,1)}), bf16[16,1,64,128]{3,2,1,0:T(8,128)(2,1)S(1)}, u32[]{:S(2)}, u32[]{:S(2)}) async-start(bf16[16,1,64,128]{3,2,1,0:T(8,128)(2,1)} %get-tuple-element.21), calls=%async_computation.1 | async-start | bytes 524288 | tf_op jit(solution)/shard_map/all_to_all | solution.py:81
  45.8 109.4 %all-reduce.3.cloned.1.call-start = ((), (), s32[]{:S(2)}) async-start(), calls=%async_computation.5 | async-start | bytes 4718592 | tf_op jit(solution)/shard_map/psum | solution.py:17
  47.5 0.7 copy-start.10
  47.5 12.1 %copy-start = (bf16[1,4096,128]{2,1,0:T(8,128)(2,1)S(1)}, bf16[1,4096,128]{2,1,0:T(8,128)(2,1)}, u32[]{:S(2)}) copy-start(bf16[1,4096,128]{2,1,0:T(8,128)(2,1)} %param.6) | copy-start | bytes 3145732
  55.7 16.4 %all-to-all-start.2 = ((bf16[16,1,64,128]{3,2,1,0:T(8,128)(2,1)}), bf16[16,1,64,128]{3,2,1,0:T(8,128)(2,1)S(1)}, u32[]{:S(2)}, u32[]{:S(2)}) async-start(bf16[16,1,64,128]{3,2,1,0:T(8,128)(2,1)} %get-tuple-element.22), calls=%async_computation.2 | async-start | bytes 524288 | tf_op jit(solution)/shard_map/all_to_all | solution.py:81
  59.3 152.3 %reduce-scatter.2.cloned.1.call-start = ((), (), s32[]{:S(2)}) async-start(), calls=%async_computation.4 | async-start | bytes 24576 | tf_op jit(solution)/shard_map/reduce_scatter | solution.py:145
  104.4 65.9 %collective-permute-start = (bf16[1,1,384,16,128]{4,3,2,1,0:T(8,128)(2,1)}, bf16[1,1,384,16,128]{4,3,2,1,0:T(8,128)(2,1)}, u32[]{:S(2)}, u32[]{:S(2)}) collective-permute-start(bf16[1,1,384,16,128]{4,3,2,1,0:T(8,128)(2,1)} %fusion.17), channel_id=1, source_target_pairs={{0,1},{1,0},{2,3},{3,2},{4,5},{5,4},{6,7},{7,6},{8,9},{9,8},{10,11... | collective-permute-start | bytes 4718600 | tf_op jit(solution)/shard_map/ppermute | solution.py:23
  155.2 1.6 copy-start.6
  156.9 1.4 copy-start.5
  156.9 2.3 %copy-start.4 = (bf16[1,384,16,128]{3,2,1,0:T(8,128)(2,1)S(1)}, bf16[1,384,16,128]{3,2,1,0:T(8,128)(2,1)}, u32[]{:S(2)}) copy-start(bf16[1,384,16,128]{3,2,1,0:T(8,128)(2,1)} %pad_maximum_fusion.2) | copy-start | bytes 4718596
  178.8 2.0 copy-start.1
  197.2 2.1 copy-start.3
  199.4 1.4 copy-start.2
Sparse Core Ops, SparseCore 0:
  50.2 104.9 all-reduce.2
  202.3 9.2 reduce-scatter.1
